TPU v7x, 32 devices: a whole 2x2x4 slice. The times are simulated.
32 devices in a mesh: blk: 8 (over z, x), group: 4 (over y, core).
Axes of the slice: x: 2, y: 2, z: 4, core: 2. Of those that a mesh axis runs over, the one named last changes fastest.
Arguments:
- activations: bfloat16 [131072, 2048], P(('blk', 'group')), may hold values from -8 to 8
- grad_out: bfloat16 [131072, 512], P(('blk', 'group')), may hold values from -8 to 8
- weights: float32 [2048, 512], P(('blk', 'group')), may hold values from -6 to 6
- momentum: float32 [2048, 512], P(('blk', 'group')), may hold values from -6 to 6
Outputs:
- new_weights: float32 [2048, 512], P(('blk', 'group'))
- new_momentum: float32 [2048, 512], P(('blk', 'group'))
All inputs are finite; a program needn't handle non-finite values.
Results may differ from a plain program's by a relative error of at most 0.0003.
Values sent between devices are 32-bit elements; how exact they have to be, the bound alone decides.
A program may use at most 128 MiB of HBM per device.

v0:
```python
import math

import jax
import jax.numpy as jnp
from jax import lax
from jax.sharding import PartitionSpec as P

epsilon = 1e-06


def swapped(value, axis, distance):
    mask = 2**distance
    pairs = [(source, source ^ mask) for source in range(lax.axis_size(axis))]
    return lax.ppermute(value, axis, pairs)


def shards(activations, grad_out, weights, momentum):
    blk_count = lax.axis_size("blk")
    group_count = lax.axis_size("group")
    levels = group_count.bit_length() - 1
    tok_rows = activations.shape[0]
    grad_scale = 1.0 / math.sqrt(tok_rows * blk_count)
    contract = (((0,), (0,)), ((), ()))
    whole_grad = (
        lax.dot_general(activations, grad_out, contract, preferred_element_type=jnp.float32)
        * grad_scale
    )
    current = lax.psum_scatter(whole_grad, "blk", scatter_dimension=0, tiled=True)
    group_index = lax.axis_index("group")
    for level_step in range(levels):
        pair_bit = levels - 1 - level_step
        half_rows = current.shape[0] // 2
        upper_side = group_index >> pair_bit & 1
        lower_half = current[:half_rows]
        upper_half = current[half_rows:]
        kept_half = jnp.where(upper_side == 1, upper_half, lower_half)
        sent_half = jnp.where(upper_side == 1, lower_half, upper_half)
        received = swapped(sent_half, "group", pair_bit)
        first_part = jnp.where(upper_side == 0, kept_half, received)
        second_part = jnp.where(upper_side == 0, received, kept_half)
        partial_value = jnp.stack(
            [
                jnp.sum(first_part * second_part),
                jnp.sum(first_part * first_part),
                jnp.sum(second_part * second_part),
            ]
        )
        sums_now = lax.psum(partial_value, "blk")
        for other_bit in range(pair_bit, levels):
            sums_now = sums_now + swapped(sums_now, "group", other_bit)
        coef_first = 1.0 - sums_now[0] / (2.0 * (sums_now[1] + epsilon))
        coef_second = 1.0 - sums_now[0] / (2.0 * (sums_now[2] + epsilon))
        current = coef_first * first_part + coef_second * second_part
    new_momentum = 0.9 * momentum + current
    new_weights = (1.0 - 0.1 * 0.1) * weights - 0.1 * new_momentum
    return (new_weights, new_momentum)


def solution(mesh):
    in_specs = (
        P(("blk", "group"), None),
        P(("blk", "group"), None),
        P(("blk", "group"), None),
        P(("blk", "group"), None),
    )
    out_specs = (P(("blk", "group"), None), P(("blk", "group"), None))
    return jax.shard_map(shards, mesh=mesh, in_specs=in_specs, out_specs=out_specs, check_vma=False)
```

profile of v0, /device:TPU:0, one launch (start us, length us, event | category | flops | bytes accessed | tf_op | source)
XLA Modules:
  0.0 190.5 jit_solution(18427046862085119366)
XLA Ops:
  7.2 0.0 reduce-scatter.2.cloned.1.call-start
  7.2 14.9 %convolution_multiply_fusion = f32[2048,512]{1,0:T(8,128)} fusion(bf16[4096,2048]{1,0:T(8,128)(2,1)} %param.4, bf16[4096,512]{1,0:T(8,128)(2,1)} %param.5), kind=kOutput, calls=%fused_computation | convolution fusion | flops 8590983168 | bytes 25165824 | tf_op jit(solution)/shard_map/dot_general | solution.py:25
  22.1 0.0 copy-start
  22.1 0.0 copy-start.1
  22.1 0.0 reduce-scatter.2.cloned.1.call-update
  22.2 91.2 %reduce-scatter.2.cloned.1.call-done = f32[256,512]{1,0:T(8,128)} async-done(((f32[2048,512]{1,0:T(8,128)}), f32[256,512]{1,0:T(8,128)}) %reduce-scatter.2.cloned.1.call-update) | async-done | bytes 524304 | tf_op jit(solution)/shard_map/reduce_scatter | solution.py:28
  113.4 1.1 slice_select_fusion
  114.4 1.5 collective-permute-start
  116.0 6.2 %collective-permute-done = f32[128,512]{1,0:T(8,128)S(1)} collective-permute-done((f32[128,512]{1,0:T(8,128)S(1)}, f32[128,512]{1,0:T(8,128)S(1)}, u32[]{:S(2)}, u32[]{:S(2)}) %collective-permute-start) | collective-permute-done | bytes 262176 | tf_op jit(solution)/shard_map/ppermute | solution.py:14
  122.2 1.8 multiply_reduce_fusion.2
  124.0 2.1 %pad_maximum_fusion = f32[3]{0:T(128)S(1)} fusion(f32[1]{0:T(128)} %bitcast.2, f32[1]{0:T(128)} %bitcast.1, f32[1]{0:T(128)} %bitcast), kind=kLoop, calls=%fused_computation.18 | loop fusion | flops 6 | bytes 24 | tf_op jit(solution)/shard_map/stack | solution.py:41
  126.0 20.6 %psum.14 = f32[3]{0:T(128)S(1)} all-reduce(f32[3]{0:T(128)S(1)} %pad_maximum_fusion), channel_id=1, replica_groups=mesh['blk'=8,'group'=4] {'blk'}, use_global_device_ids=true, to_apply=%region_4.5 | all-reduce | flops 3 | bytes 24 | tf_op jit(solution)/shard_map/psum | solution.py:48
  146.7 1.5 collective-permute-start.1
  148.2 2.1 %collective-permute-done.1 = f32[3]{0:T(128)S(1)} collective-permute-done((f32[3]{0:T(128)S(1)}, f32[3]{0:T(128)S(1)}, u32[]{:S(2)}, u32[]{:S(2)}) %collective-permute-start.1) | collective-permute-done | bytes 44 | tf_op jit(solution)/shard_map/ppermute | solution.py:14
  150.3 0.7 fusion.1
  153.7 0.1 collective-permute-start.2
  153.8 1.3 collective-permute-done.2
  155.1 0.7 multiply_reduce_fusion.5
  155.9 2.1 %pad_maximum_fusion.1 = f32[3]{0:T(128)S(1)} fusion(f32[1]{0:T(128)} %bitcast.7, f32[1]{0:T(128)} %bitcast.6, f32[1]{0:T(128)} %bitcast.5), kind=kLoop, calls=%fused_computation.19 | loop fusion | flops 6 | bytes 24 | tf_op jit(solution)/shard_map/stack | solution.py:41
  157.9 17.1 %psum.15 = f32[3]{0:T(128)S(1)} all-reduce(f32[3]{0:T(128)S(1)} %pad_maximum_fusion.1), channel_id=1, replica_groups=mesh['blk'=8,'group'=4] {'blk'}, use_global_device_ids=true, to_apply=%region_8.9 | all-reduce | flops 3 | bytes 24 | tf_op jit(solution)/shard_map/psum | solution.py:48
  175.1 0.1 collective-permute-start.3
  175.1 1.1 collective-permute-done.3
  176.3 1.5 collective-permute-start.4
  177.8 2.1 %collective-permute-done.4 = f32[3]{0:T(128)S(1)} collective-permute-done((f32[3]{0:T(128)S(1)}, f32[3]{0:T(128)S(1)}, u32[]{:S(2)}, u32[]{:S(2)}) %collective-permute-start.4) | collective-permute-done | bytes 44 | tf_op jit(solution)/shard_map/ppermute | solution.py:14
  179.8 0.6 fusion
  182.9 0.0 copy-done
  182.9 0.0 copy-done.1
  182.9 0.7 multiply_subtract_fusion
  (5 shorter events, 0.1 us)
Async XLA Ops:
  7.2 106.2 %reduce-scatter.2.cloned.1.call-start = ((), (), s32[]{:S(2)}) async-start(), calls=%async_computation.1 | async-start | bytes 4718592 | tf_op jit(solution)/shard_map/reduce_scatter | solution.py:28
  22.1 160.7 %copy-start = (f32[64,512]{1,0:T(8,128)S(1)}, f32[64,512]{1,0:T(8,128)}, u32[]{:S(2)}) copy-start(f32[64,512]{1,0:T(8,128)} %param.6) | copy-start | bytes 393220
  22.1 160.7 %copy-start.1 = (f32[64,512]{1,0:T(8,128)S(1)}, f32[64,512]{1,0:T(8,128)}, u32[]{:S(2)}) copy-start(f32[64,512]{1,0:T(8,128)} %param.7) | copy-start | bytes 393220
  114.4 7.7 %collective-permute-start = (f32[128,512]{1,0:T(8,128)S(1)}, f32[128,512]{1,0:T(8,128)S(1)}, u32[]{:S(2)}, u32[]{:S(2)}) collective-permute-start(f32[128,512]{1,0:T(8,128)S(1)} %slice_select_fusion), channel_id=1, source_target_pairs={{0,2},{1,3},{2,0},{3,1},{4,6},{5,7},{6,4},{7,5},{8,10},{9,11},{10,... | collective-permute-start | bytes 786440 | tf_op jit(solution)/shard_map/ppermute | solution.py:14
  146.7 3.6 %collective-permute-start.1 = (f32[3]{0:T(128)S(1)}, f32[3]{0:T(128)S(1)}, u32[]{:S(2)}, u32[]{:S(2)}) collective-permute-start(f32[3]{0:T(128)S(1)} %psum.14), channel_id=1, source_target_pairs={{0,2},{1,3},{2,0},{3,1},{4,6},{5,7},{6,4},{7,5},{8,10},{9,11},{10,... | collective-permute-start | bytes 44 | tf_op jit(solution)/shard_map/ppermute | solution.py:14
  153.7 1.4 collective-permute-start.2
  175.1 1.2 collective-permute-start.3
  176.3 3.6 %collective-permute-start.4 = (f32[3]{0:T(128)S(1)}, f32[3]{0:T(128)S(1)}, u32[]{:S(2)}, u32[]{:S(2)}) collective-permute-start(f32[3]{0:T(128)S(1)} %add.44), channel_id=1, source_target_pairs={{0,2},{1,3},{2,0},{3,1},{4,6},{5,7},{6,4},{7,5},{8,10},{9,11},{10,... | collective-permute-start | bytes 44 | tf_op jit(solution)/shard_map/ppermute | solution.py:14
Sparse Core Ops, SparseCore 0:
  22.3 91.0 reduce-scatter.1
where the time goes:
time: 191 us; the launch traced here: 190 us
  waiting for transfers between devices  104 us (54%)
  blocking collectives  37.7 us (20%)
  between operations  19.2 us (10%)
  matrix products  14.9 us (8%)
  other arithmetic  8.55 us (4%)
  starting transfers between devices  4.72 us (2%)
    reduce_scatter x1, waiting for transfers between devices, shards(): lax.psum_scatter(whole_grad, 'blk', scatter_dimension=0, tiled=True)  91.2 us
    psum x2, blocking collectives, shards(): sums_now = lax.psum(partial_value, 'blk')  37.7 us
    dot_general x1, matrix products, shards(): lax.dot_general(activations, grad_out, contract, preferred_element_type=j...  14.9 us
    ppermute x5, waiting for transfers between devices, swapped(): return lax.ppermute(value, axis, pairs)  12.8 us
    ppermute x5, starting transfers between devices, swapped(): return lax.ppermute(value, axis, pairs)  4.68 us
    another operation x2, other arithmetic, shards(): jnp.stack([jnp.sum(first_part * second_part), jnp.sum(first_part * first_...  4.11 us
  transfers between devices with their start and end apart: 6, of which 6 were waited for; matrix products, arithmetic and copies ran while one was open for 0% of the time, Pallas kernels for 0%

commit v1 on v0

v1 whole, which is shorter than its diff:
```python
import functools
import math

import jax
import jax.numpy as jnp
from jax import lax
from jax.experimental import pallas as pl
from jax.experimental.pallas import tpu as pltpu
from jax.sharding import PartitionSpec as P

epsilon = 1e-06
MESH = pl.DeviceIdType.MESH
PIECES = 4
FIRST_EVENT_STEP = 3


def flipped(index, mask, bits):
    for bit in range(bits):
        if mask >> bit & 1:
            weight = 1 << bit
            index = index + weight * (1 - 2 * lax.rem(lax.div(index, weight), 2))
    return index


class Plan:
    def __init__(self, blk_count, group_count):
        self.blk_count, self.group_count = blk_count, group_count
        self.blk_bits = blk_count.bit_length() - 1
        self.group_bits = group_count.bit_length() - 1
        self.hs = list(range(group_count - 1, -1, -1))
        self.slots = {}
        for h in self.hs:
            for r in range(blk_count):
                for stage in self.receives(r, h):
                    self.slots[stage, r, h] = len(self.slots)

    def order(self, h):
        return list(range(self.blk_bits))

    def receives(self, r, h):
        sent = self.sends(r, h)
        return range(self.blk_bits if sent is None else sent[0])

    def sends(self, r, h):
        for stage, bit in enumerate(self.order(h)):
            if r >> bit & 1:
                return stage, bit
        return None

    def pairs(self):
        return [(k, l) for k in range(self.group_count) for l in range(k, self.group_count)]


def kernel(
    plan, grad_scale, act_ref, gout_ref, out_ref,
    act_buf, gout_buf, acc, arrived, pieces, gram_own, gram_sum, gram_group, gram_blk,
    act_sem, gout_sem, send_sem, recv_sem, gsend_sem, grecv_sem,
    asend_sem, arecv_sem, bsend_sem, brecv_sem,
):
    b = lax.axis_index("blk")
    g = lax.axis_index("group")
    B, G = plan.blk_count, plan.group_count
    tokens = act_ref.shape[0]
    blk_rows = acc.shape[1] * acc.shape[2]
    cols = acc.shape[3]
    depth = tokens // PIECES
    b_of = [flipped(b, r, plan.blk_bits) for r in range(B)]
    g_of = [flipped(g, h, plan.group_bits) for h in range(G)]

    def act_copy(r, piece):
        rows = pl.ds(pl.multiple_of(piece * depth, depth), depth)
        lanes = pl.ds(pl.multiple_of(b_of[r] * blk_rows, blk_rows), blk_rows)
        return pltpu.make_async_copy(
            act_ref.at[rows, lanes], act_buf.at[r, rows], act_sem.at[r, piece]
        )

    def gout_copy(piece):
        rows = pl.ds(pl.multiple_of(piece * depth, depth), depth)
        return pltpu.make_async_copy(gout_ref.at[rows], gout_buf.at[rows], gout_sem.at[piece])

    for piece in range(PIECES):
        gout_copy(piece).start()
        act_copy(B - 1, piece).start()
    for r in range(B - 2, -1, -1):
        for piece in range(PIECES):
            act_copy(r, piece).start()

    barrier = pltpu.get_barrier_semaphore()
    for r in range(1, B):
        pl.semaphore_signal(barrier, inc=1, device_id=(b_of[r], g), device_id_type=MESH)
    for h in range(1, G):
        pl.semaphore_signal(barrier, inc=1, device_id=(b, g_of[h]), device_id_type=MESH)

    def matmul(r):
        def step(piece, first):
            act_copy(r, piece).wait()
            if r == B - 1:
                gout_copy(piece).wait()
            rows = pl.ds(pl.multiple_of(piece * depth, depth), depth)
            product = lax.dot_general(
                act_buf[r, rows], gout_buf[rows], (((0,), (0,)), ((), ())),
                preferred_element_type=jnp.float32,
            ).reshape(acc.shape[1:])
            if first:
                acc[r] = product
            else:
                acc[r] += product

        step(0, True)

        def body(piece, carry):
            step(piece, False)
            return carry

        lax.fori_loop(1, PIECES, body, 0)

    def block_copy(slot_key):
        stage, r, h = slot_key
        slot = plan.slots[slot_key]
        mask = 1 << plan.order(h)[stage]
        return pltpu.make_async_remote_copy(
            src_ref=acc.at[r ^ mask, g_of[h]],
            dst_ref=arrived.at[slot],
            send_sem=send_sem.at[slot],
            recv_sem=recv_sem.at[slot],
            device_id=(b_of[mask], g),
            device_id_type=MESH,
        )

    def group_copy(h):
        return pltpu.make_async_remote_copy(
            src_ref=acc.at[0, g_of[h]],
            dst_ref=pieces.at[h],
            send_sem=gsend_sem.at[h],
            recv_sem=grecv_sem.at[h],
            device_id=(b, g_of[h]),
            device_id_type=MESH,
        )

    def send(r, h):
        stage, bit = plan.sends(r, h)
        block_copy((stage, r ^ (1 << bit), h)).start()

    def process(r, h):
        keys = [(stage, r, h) for stage in plan.receives(r, h)]
        total = acc[r, g_of[h]]
        for key in keys:
            block_copy(key).wait_recv()
            total = total + arrived[plan.slots[key]]
        if r:
            acc[r, g_of[h]] = total
            send(r, h)
        elif h:
            acc[0, g_of[h]] = total * grad_scale
            group_copy(h).start()
        else:
            pieces[0] = total * grad_scale

    pending = []
    for step in range(B):
        r = B - 1 - step
        matmul(r)
        if step == 0:
            pl.semaphore_wait(barrier, B - 1 + G - 1)
        for h in plan.hs:
            if len(plan.receives(r, h)) == 0:
                send(r, h)
            else:
                pending.append((r, h))
        if step >= FIRST_EVENT_STEP and step < B - 1:
            process(*pending.pop(0))
    for r, h in pending:
        process(r, h)

    for h in range(1, G):
        group_copy(h).wait_recv()
    pairs = plan.pairs()
    place = [flipped(g, k, plan.group_bits) for k in range(G)]
    for at, (k, l) in enumerate(pairs):
        gram_own[pl.ds(at, 1), :] = jnp.sum(
            jnp.sum(pieces[place[k]] * pieces[place[l]], axis=0, keepdims=True).reshape(1, cols // 128, 128),
            axis=1,
        )
    for at in range(len(pairs), gram_own.shape[0]):
        gram_own[pl.ds(at, 1), :] = jnp.zeros((1, 128), jnp.float32)

    def gram_copy_group(h):
        return pltpu.make_async_remote_copy(
            src_ref=gram_own, dst_ref=gram_group.at[h],
            send_sem=asend_sem.at[h], recv_sem=arecv_sem.at[h],
            device_id=(b, g_of[h]), device_id_type=MESH,
        )

    def gram_copy_blk(r):
        return pltpu.make_async_remote_copy(
            src_ref=gram_sum, dst_ref=gram_blk.at[r],
            send_sem=bsend_sem.at[r], recv_sem=brecv_sem.at[r],
            device_id=(b_of[r], g), device_id_type=MESH,
        )

    for h in range(G - 1, 0, -1):
        gram_copy_group(h).start()
    total = gram_own[...]
    for h in range(1, G):
        gram_copy_group(h).wait_recv()
        total = total + gram_group[h]
    gram_sum[...] = total
    for r in range(B - 1, 0, -1):
        gram_copy_blk(r).start()
    for r in range(1, B):
        gram_copy_blk(r).wait_recv()
        total = total + gram_blk[r]
    sums = jnp.sum(total, axis=1, keepdims=True)
    gram = {}
    for at, (k, l) in enumerate(pairs):
        gram[k, l] = gram[l, k] = sums[at:at + 1]

    def product(first, second):
        result = None
        for k, weight in first.items():
            inner = None
            for l, other in second.items():
                term = gram[k, l] if other is None else other * gram[k, l]
                inner = term if inner is None else inner + term
            inner = inner if weight is None else weight * inner
            result = inner if result is None else result + inner
        return result

    entries = [{k: None} for k in range(G)]
    while len(entries) > 1:
        half = len(entries) // 2
        merged = []
        for i in range(half):
            first, second = entries[i], entries[i + half]
            inner = product(first, second)
            first_sq = jnp.maximum(product(first, first), 0.0)
            second_sq = jnp.maximum(product(second, second), 0.0)
            coef_first = 1.0 - inner / (2.0 * (first_sq + epsilon))
            coef_second = 1.0 - inner / (2.0 * (second_sq + epsilon))
            entry = {}
            for source, coef in ((first, coef_first), (second, coef_second)):
                for k, weight in source.items():
                    entry[k] = coef if weight is None else coef * weight
            merged.append(entry)
        entries = merged
    combined = None
    for k, weight in entries[0].items():
        term = weight * pieces[place[k]]
        combined = term if combined is None else combined + term
    out_ref[...] = combined

    for key in plan.slots:
        block_copy(key).wait_send()
    for h in range(1, G):
        group_copy(h).wait_send()
        gram_copy_group(h).wait_send()
    for r in range(1, B):
        gram_copy_blk(r).wait_send()


def shards(blk_count, group_count, activations, grad_out, weights, momentum):
    plan = Plan(blk_count, group_count)
    tok_rows, width = activations.shape
    cols = grad_out.shape[1]
    sub_rows = width // (blk_count * group_count)
    blk_rows = sub_rows * group_count
    grad_scale = 1.0 / math.sqrt(tok_rows * blk_count)
    gram_rows = -(-len(plan.pairs()) // 8) * 8
    dma = pltpu.SemaphoreType.DMA
    f32 = jnp.float32
    combined = pl.pallas_call(
        functools.partial(kernel, plan, grad_scale),
        out_shape=jax.ShapeDtypeStruct((sub_rows, cols), f32),
        in_specs=[pl.BlockSpec(memory_space=pl.ANY)] * 2,
        out_specs=pl.BlockSpec(memory_space=pltpu.VMEM),
        scratch_shapes=[
            pltpu.VMEM((blk_count, tok_rows, blk_rows), activations.dtype),
            pltpu.VMEM((tok_rows, cols), grad_out.dtype),
            pltpu.VMEM((blk_count, group_count, sub_rows, cols), f32),
            pltpu.VMEM((len(plan.slots), sub_rows, cols), f32),
            pltpu.VMEM((group_count, sub_rows, cols), f32),
            pltpu.VMEM((gram_rows, 128), f32),
            pltpu.VMEM((gram_rows, 128), f32),
            pltpu.VMEM((group_count, gram_rows, 128), f32),
            pltpu.VMEM((blk_count, gram_rows, 128), f32),
            dma((blk_count, PIECES)),
            dma((PIECES,)),
            dma((len(plan.slots),)),
            dma((len(plan.slots),)),
            dma((group_count,)),
            dma((group_count,)),
            dma((group_count,)),
            dma((group_count,)),
            dma((blk_count,)),
            dma((blk_count,)),
        ],
        compiler_params=pltpu.CompilerParams(
            collective_id=0, has_side_effects=True, vmem_limit_bytes=50 * 1024 * 1024
        ),
        name="adasum",
    )(activations, grad_out)
    new_momentum = 0.9 * momentum + combined
    new_weights = (1.0 - 0.1 * 0.1) * weights - 0.1 * new_momentum
    return (new_weights, new_momentum)


def solution(mesh):
    spec = P(("blk", "group"), None)
    body = functools.partial(shards, mesh.shape["blk"], mesh.shape["group"])
    return jax.shard_map(
        body, mesh=mesh, in_specs=(spec,) * 4, out_specs=(spec,) * 2, check_vma=False
    )
```

time: 191 us -> 70.2 us (0.37)
  waiting for transfers between devices: 104 us -> 0 us
  Pallas kernels: 0 us -> 68.7 us
  blocking collectives: 37.7 us -> 0 us
  between operations: 19.2 us -> 0.67 us
  matrix products: 14.9 us -> 0 us
  other arithmetic: 8.55 us -> 0.74 us
  starting transfers between devices: 4.72 us -> 0 us
    reduce_scatter x1 -> x0, waiting for transfers between devices: 91.2 us -> none  [shards(): lax.psum_scatter(whole_grad, 'blk', scatter_dimension=0, tiled=True)]
    pallas_call x0 -> x1, Pallas kernels: none -> 68.7 us  [shards(): pl.pallas_call(functools.partial(kernel, plan, grad_scale), out_shape=jax...]
    psum x2 -> x0, blocking collectives: 37.7 us -> none  [shards(): sums_now = lax.psum(partial_value, 'blk')]
    dot_general x1 -> x0, matrix products: 14.9 us -> none  [shards(): lax.dot_general(activations, grad_out, contract, preferred_element_type=j...]
    ppermute x5 -> x0, waiting for transfers between devices: 12.8 us -> none  [swapped(): return lax.ppermute(value, axis, pairs)]
    ppermute x5 -> x0, starting transfers between devices: 4.68 us -> none  [swapped(): return lax.ppermute(value, axis, pairs)]
    another operation x2 -> x0, other arithmetic: 4.11 us -> none  [shards(): jnp.stack([jnp.sum(first_part * second_part), jnp.sum(first_part * first_...]
    reduce_sum x2 -> x0, other arithmetic: 2.55 us -> none  [shards(): jnp.sum(first_part * second_part)]
  transfers between devices with their start and end apart: 6 -> 0, of which waited for: 6 -> 0; matrix products, arithmetic and copies ran while one was open for 0% -> 0% of each run, Pallas kernels for 0% -> 0%
where the time goes in v1:
time: 70.2 us; the launch traced here: 70.1 us
  Pallas kernels  68.7 us (98%)
  other arithmetic  0.74 us (1%)
    pallas_call x1, Pallas kernels, shards(): pl.pallas_call(functools.partial(kernel, plan, grad_scale), out_shape=jax...  68.7 us

profile of v1, /device:TPU:0, one launch (start us, length us, event | category | flops | bytes accessed | tf_op | source)
XLA Modules:
  0.0 70.1 jit_solution(3071227796780776093)
XLA Ops:
  0.6 0.0 copy-start.1
  0.6 0.0 copy-start
  0.7 68.7 %adasum.1 = f32[64,512]{1,0:T(8,128)S(1)} custom-call(bf16[4096,2048]{1,0:T(8,128)(2,1)} %act_ref.1, bf16[4096,512]{1,0:T(8,128)(2,1)} %gout_ref.1), custom_call_target="tpu_custom_call" | custom-call | tf_op jit(solution)/shard_map/adasum/pallas_call | solution.py:271
  69.3 0.0 copy-done.1
  69.4 0.0 copy-done
  69.4 0.7 %multiply_subtract_fusion = (f32[64,512]{1,0:T(8,128)}, f32[64,512]{1,0:T(8,128)}) fusion(f32[64,512]{1,0:T(8,128)S(1)} %copy-done, f32[64,512]{1,0:T(8,128)S(1)} %adasum.1, f32[64,512]{1,0:T(8,128)S(1)} %copy-done.1), kind=kLoop, calls=%fused_computation | loop fusion | flops 163840 | bytes 655360 | tf_op jit(solution)/shard_map/sub | solution.py:303
Async XLA Ops:
  0.6 68.7 %copy-start.1 = (f32[64,512]{1,0:T(8,128)S(1)}, f32[64,512]{1,0:T(8,128)}, u32[]{:S(2)}) copy-start(f32[64,512]{1,0:T(8,128)} %param.7) | copy-start | bytes 393220
  0.6 68.7 %copy-start = (f32[64,512]{1,0:T(8,128)S(1)}, f32[64,512]{1,0:T(8,128)}, u32[]{:S(2)}) copy-start(f32[64,512]{1,0:T(8,128)} %param.6) | copy-start | bytes 393220

commit v2 on v1

--- a/solution.py
+++ b/solution.py
@@ -28,6 +28,7 @@
         self.blk_bits = blk_count.bit_length() - 1
         self.group_bits = group_count.bit_length() - 1
         self.hs = list(range(group_count - 1, -1, -1))
+        self.mixed = blk_count == 8
         self.slots = {}
         for h in self.hs:
             for r in range(blk_count):
@@ -35,7 +36,10 @@
                     self.slots[stage, r, h] = len(self.slots)
 
     def order(self, h):
-        return list(range(self.blk_bits))
+        bits = list(range(self.blk_bits))
+        if self.mixed and h == self.hs[0]:
+            bits[:2] = bits[1::-1]
+        return bits
 
     def receives(self, r, h):
         sent = self.sends(r, h)
@@ -46,6 +50,56 @@
             if r >> bit & 1:
                 return stage, bit
         return None
+
+    def schedule(self):
+        if self.mixed:
+            return self.mixed_schedule()
+        steps, pending = [], []
+        for r in range(self.blk_count - 1, -1, -1):
+            steps.append(("matmul", r, None))
+            for h in self.hs:
+                if len(self.receives(r, h)) == 0:
+                    steps.append(("send", r, h))
+                else:
+                    pending.append(("process", r, h))
+            if r < self.blk_count - FIRST_EVENT_STEP and r > 0:
+                steps.append(pending.pop(0))
+        return steps + pending
+
+    def mixed_schedule(self):
+        steps = []
+        first, rest = self.hs[0], self.hs[1:]
+
+        def matmul(r):
+            steps.append(("matmul", r, None))
+
+        def add(kind, r, hs):
+            steps.extend((kind, r, h) for h in hs)
+
+        matmul(7)
+        add("send", 7, [first] + rest)
+        matmul(6)
+        add("send", 6, [first])
+        matmul(3)
+        add("send", 3, [first])
+        matmul(5)
+        add("send", 5, rest)
+        add("process", 5, [first])
+        add("send", 3, rest)
+        add("process", 6, rest[:1])
+        matmul(2)
+        add("send", 2, [first])
+        matmul(1)
+        add("process", 6, rest[1:2])
+        add("process", 1, [first])
+        add("send", 1, rest)
+        matmul(4)
+        add("process", 6, rest[2:])
+        matmul(0)
+        add("process", 4, [first] + rest)
+        add("process", 2, rest)
+        add("process", 0, [first] + rest)
+        return steps
 
     def pairs(self):
         return [(k, l) for k in range(self.group_count) for l in range(k, self.group_count)]
@@ -78,12 +132,17 @@
         rows = pl.ds(pl.multiple_of(piece * depth, depth), depth)
         return pltpu.make_async_copy(gout_ref.at[rows], gout_buf.at[rows], gout_sem.at[piece])
 
+    steps = plan.schedule()
+    loads = [r for kind, r, h in steps if kind == "matmul"]
+
+    def prefetch(at):
+        if at < B:
+            for piece in range(PIECES):
+                act_copy(loads[at], piece).start()
+
     for piece in range(PIECES):
         gout_copy(piece).start()
-        act_copy(B - 1, piece).start()
-    for r in range(B - 2, -1, -1):
-        for piece in range(PIECES):
-            act_copy(r, piece).start()
+        act_copy(loads[0], piece).start()
 
     barrier = pltpu.get_barrier_semaphore()
     for r in range(1, B):
@@ -94,7 +153,7 @@
     def matmul(r):
         def step(piece, first):
             act_copy(r, piece).wait()
-            if r == B - 1:
+            if r == loads[0]:
                 gout_copy(piece).wait()
             rows = pl.ds(pl.multiple_of(piece * depth, depth), depth)
             product = lax.dot_general(
@@ -107,6 +166,8 @@
                 acc[r] += product
 
         step(0, True)
+        if r == loads[0]:
+            prefetch(1)
 
         def body(piece, carry):
             step(piece, False)
@@ -156,21 +217,19 @@
         else:
             pieces[0] = total * grad_scale
 
-    pending = []
-    for step in range(B):
-        r = B - 1 - step
-        matmul(r)
-        if step == 0:
-            pl.semaphore_wait(barrier, B - 1 + G - 1)
-        for h in plan.hs:
-            if len(plan.receives(r, h)) == 0:
-                send(r, h)
-            else:
-                pending.append((r, h))
-        if step >= FIRST_EVENT_STEP and step < B - 1:
-            process(*pending.pop(0))
-    for r, h in pending:
-        process(r, h)
+    done = 0
+    for kind, r, h in steps:
+        if kind == "matmul":
+            if done:
+                prefetch(done + 1)
+            matmul(r)
+            done += 1
+            if done == 1:
+                pl.semaphore_wait(barrier, B - 1 + G - 1)
+        elif kind == "send":
+            send(r, h)
+        else:
+            process(r, h)
 
     for h in range(1, G):
         group_copy(h).wait_recv()

time: 70.2 us -> 62.1 us (0.88)
  Pallas kernels: 68.7 us -> 60.6 us
    pallas_call x1, Pallas kernels: 68.7 us -> 60.6 us  [shards(): pl.pallas_call(functools.partial(kernel, plan, grad_scale), out_shape=jax...]
where the time goes in v2:
time: 62.1 us; the launch traced here: 62 us
  Pallas kernels  60.6 us (98%)
  other arithmetic  0.74 us (1%)
  between operations  0.67 us (1%)
    pallas_call x1, Pallas kernels, shards(): pl.pallas_call(functools.partial(kernel, plan, grad_scale), out_shape=jax...  60.6 us

profile of v2, /device:TPU:0, one launch (start us, length us, event | category | flops | bytes accessed | tf_op | source)
XLA Modules:
  0.0 62.0 jit_solution(11026059171385598587)
XLA Ops:
  0.6 0.0 copy-start.1
  0.6 0.0 copy-start
  0.7 60.6 %adasum.1 = f32[64,512]{1,0:T(8,128)S(1)} custom-call(bf16[4096,2048]{1,0:T(8,128)(2,1)} %act_ref.1, bf16[4096,512]{1,0:T(8,128)(2,1)} %gout_ref.1), custom_call_target="tpu_custom_call" | custom-call | tf_op jit(solution)/shard_map/adasum/pallas_call | solution.py:330
  61.2 0.0 copy-done.1
  61.2 0.0 copy-done
  61.3 0.7 %multiply_subtract_fusion = (f32[64,512]{1,0:T(8,128)}, f32[64,512]{1,0:T(8,128)}) fusion(f32[64,512]{1,0:T(8,128)S(1)} %copy-done, f32[64,512]{1,0:T(8,128)S(1)} %adasum.1, f32[64,512]{1,0:T(8,128)S(1)} %copy-done.1), kind=kLoop, calls=%fused_computation | loop fusion | flops 163840 | bytes 655360 | tf_op jit(solution)/shard_map/sub | solution.py:362
Async XLA Ops:
  0.6 60.6 %copy-start.1 = (f32[64,512]{1,0:T(8,128)S(1)}, f32[64,512]{1,0:T(8,128)}, u32[]{:S(2)}) copy-start(f32[64,512]{1,0:T(8,128)} %param.7) | copy-start | bytes 393220
  0.6 60.6 %copy-start = (f32[64,512]{1,0:T(8,128)S(1)}, f32[64,512]{1,0:T(8,128)}, u32[]{:S(2)}) copy-start(f32[64,512]{1,0:T(8,128)} %param.6) | copy-start | bytes 393220

commit v3 on v2

--- a/solution.py
+++ b/solution.py
@@ -96,7 +96,7 @@
         matmul(4)
         add("process", 6, rest[2:])
         matmul(0)
-        add("process", 4, [first] + rest)
+        add("process", 4, rest[:2] + [first] + rest[2:])
         add("process", 2, rest)
         add("process", 0, [first] + rest)
         return steps
@@ -235,13 +235,12 @@
         group_copy(h).wait_recv()
     pairs = plan.pairs()
     place = [flipped(g, k, plan.group_bits) for k in range(G)]
+    lane = lax.broadcasted_iota(jnp.int32, gram_own.shape, 1)
+    total = jnp.zeros(gram_own.shape, jnp.float32)
     for at, (k, l) in enumerate(pairs):
-        gram_own[pl.ds(at, 1), :] = jnp.sum(
-            jnp.sum(pieces[place[k]] * pieces[place[l]], axis=0, keepdims=True).reshape(1, cols // 128, 128),
-            axis=1,
-        )
-    for at in range(len(pairs), gram_own.shape[0]):
-        gram_own[pl.ds(at, 1), :] = jnp.zeros((1, 128), jnp.float32)
+        inner = jnp.sum(pieces[place[k]] * pieces[place[l]], axis=0, keepdims=True)
+        total = total + jnp.where(lane == at, jnp.sum(inner, axis=1, keepdims=True), 0.0)
+    gram_own[...] = total
 
     def gram_copy_group(h):
         return pltpu.make_async_remote_copy(
@@ -259,7 +258,6 @@
 
     for h in range(G - 1, 0, -1):
         gram_copy_group(h).start()
-    total = gram_own[...]
     for h in range(1, G):
         gram_copy_group(h).wait_recv()
         total = total + gram_group[h]
@@ -269,10 +267,11 @@
     for r in range(1, B):
         gram_copy_blk(r).wait_recv()
         total = total + gram_blk[r]
-    sums = jnp.sum(total, axis=1, keepdims=True)
     gram = {}
     for at, (k, l) in enumerate(pairs):
-        gram[k, l] = gram[l, k] = sums[at:at + 1]
+        gram[k, l] = gram[l, k] = jnp.sum(
+            jnp.where(lane == at, total, 0.0), axis=1, keepdims=True
+        )
 
     def product(first, second):
         result = None
@@ -324,7 +323,7 @@
     sub_rows = width // (blk_count * group_count)
     blk_rows = sub_rows * group_count
     grad_scale = 1.0 / math.sqrt(tok_rows * blk_count)
-    gram_rows = -(-len(plan.pairs()) // 8) * 8
+    gram_lanes = -(-len(plan.pairs()) // 128) * 128
     dma = pltpu.SemaphoreType.DMA
     f32 = jnp.float32
     combined = pl.pallas_call(
@@ -338,10 +337,10 @@
             pltpu.VMEM((blk_count, group_count, sub_rows, cols), f32),
             pltpu.VMEM((len(plan.slots), sub_rows, cols), f32),
             pltpu.VMEM((group_count, sub_rows, cols), f32),
-            pltpu.VMEM((gram_rows, 128), f32),
-            pltpu.VMEM((gram_rows, 128), f32),
-            pltpu.VMEM((group_count, gram_rows, 128), f32),
-            pltpu.VMEM((blk_count, gram_rows, 128), f32),
+            pltpu.VMEM((1, gram_lanes), f32),
+            pltpu.VMEM((1, gram_lanes), f32),
+            pltpu.VMEM((group_count, 1, gram_lanes), f32),
+            pltpu.VMEM((blk_count, 1, gram_lanes), f32),
             dma((blk_count, PIECES)),
             dma((PIECES,)),
             dma((len(plan.slots),)),

time: 62.1 us -> 59.1 us (0.952)
  Pallas kernels: 60.6 us -> 57.6 us
    pallas_call x1, Pallas kernels: 60.6 us -> 57.6 us  [shards(): pl.pallas_call(functools.partial(kernel, plan, grad_scale), out_shape=jax...]
where the time goes in v3:
time: 59.1 us; the launch traced here: 59 us
  Pallas kernels  57.6 us (97%)
  other arithmetic  0.74 us (1%)
  between operations  0.67 us (1%)
    pallas_call x1, Pallas kernels, shards(): pl.pallas_call(functools.partial(kernel, plan, grad_scale), out_shape=jax...  57.6 us

profile of v3, /device:TPU:0, one launch (start us, length us, event | category | flops | bytes accessed | tf_op | source)
XLA Modules:
  0.0 59.0 jit_solution(17534977430725407188)
XLA Ops:
  0.6 0.0 copy-start.1
  0.6 0.0 copy-start
  0.7 57.6 %adasum.1 = f32[64,512]{1,0:T(8,128)S(1)} custom-call(bf16[4096,2048]{1,0:T(8,128)(2,1)} %act_ref.1, bf16[4096,512]{1,0:T(8,128)(2,1)} %gout_ref.1), custom_call_target="tpu_custom_call" | custom-call | tf_op jit(solution)/shard_map/adasum/pallas_call | solution.py:329
  58.2 0.0 copy-done.1
  58.2 0.0 copy-done
  58.2 0.7 %multiply_subtract_fusion = (f32[64,512]{1,0:T(8,128)}, f32[64,512]{1,0:T(8,128)}) fusion(f32[64,512]{1,0:T(8,128)S(1)} %copy-done, f32[64,512]{1,0:T(8,128)S(1)} %adasum.1, f32[64,512]{1,0:T(8,128)S(1)} %copy-done.1), kind=kLoop, calls=%fused_computation | loop fusion | flops 163840 | bytes 655360 | tf_op jit(solution)/shard_map/sub | solution.py:361
Async XLA Ops:
  0.6 57.6 %copy-start.1 = (f32[64,512]{1,0:T(8,128)S(1)}, f32[64,512]{1,0:T(8,128)}, u32[]{:S(2)}) copy-start(f32[64,512]{1,0:T(8,128)} %param.7) | copy-start | bytes 393220
  0.6 57.6 %copy-start = (f32[64,512]{1,0:T(8,128)S(1)}, f32[64,512]{1,0:T(8,128)}, u32[]{:S(2)}) copy-start(f32[64,512]{1,0:T(8,128)} %param.6) | copy-start | bytes 393220
